TPU v7x, 256 devices: a whole 4x4x8 slice. The times are simulated.
256 devices in a mesh: layer: 8 (over x, core), feat: 32 (over y, z).
Axes of the slice: x: 4, y: 4, z: 8, core: 2. Of those that a mesh axis runs over, the one named last changes fastest.
Arguments:
- gradient: bfloat16 [8, 2560, 2560], P('layer', 'feat'), may hold values from -3 to 3
- in_inverse: bfloat16 [8, 2560, 2560], P('layer', 'feat'), may hold values from -1 to 2.5, as said below
- in_coupling: bfloat16 [8, 2560, 2560], P('layer', 'feat'), may hold values from -0.125 to 0.125
- in_carry: bfloat16 [8, 2560, 2560], P('layer', 'feat'), may hold values from -0.125 to 0.125
- out_inverse: bfloat16 [8, 20, 128, 128], P('layer'), may hold values from -1 to 2.5, as said below
- out_coupling: bfloat16 [8, 20, 128, 128], P('layer'), may hold values from -0.5 to 0.5
Outputs:
- update: bfloat16 [8, 2560, 2560], P('layer', 'feat')
Inputs may be any that keep to these rules, and one draw needn't show every extreme that they name: `in_inverse`: symmetric in its last two dimensions. `out_inverse`: symmetric in its last two dimensions.
All inputs are finite; a program needn't handle non-finite values.
Results may differ from a plain program's by a relative error of at most 0.006.
Values may be sent and summed in bfloat16 or wider, within the bound.
No kernel may reach another device: no remote copies, remote signals or barrier semaphores. Data moves between devices by JAX's collectives and lax.ppermute only.
A program may use at most 64 MiB of HBM per device.

v0:
```python
import jax
import jax.numpy as jnp
from jax import lax
from jax.sharding import PartitionSpec as P


def from_behind(x, axis, by):
    size = lax.axis_size(axis)
    pairs = [(i, i + by) for i in range(size) if 0 <= i + by < size]
    return lax.ppermute(x, axis, pairs)


def block_apply(matrix, table, flipped):
    row_count = matrix.shape[0]
    blocks = table.shape[0]
    block_width = table.shape[1]
    grouped = matrix.reshape(row_count, blocks, block_width)
    pattern = "rnb,ncb->rnc" if flipped else "rnb,nbc->rnc"
    product = jnp.einsum(pattern, grouped, table, preferred_element_type=jnp.float32)
    return product.reshape(row_count, blocks * block_width)


def contract_rows(factor, piece):
    return jnp.dot(factor, piece, preferred_element_type=jnp.float32)


def local(gradient, in_inverse, in_coupling, in_carry, out_inverse, out_coupling):
    grad_rows = gradient[0]
    inverse_rows = in_inverse[0]
    coupling_rows = in_coupling[0]
    carry_rows = in_carry[0]
    out_inv = out_inverse[0]
    out_psi = out_coupling[0]
    psi_from_below = from_behind(out_psi, "layer", 1)
    from_above = from_behind(grad_rows, "layer", -1)
    near_rows = block_apply(from_above, out_psi, True).astype(jnp.bfloat16)
    coupled = contract_rows(coupling_rows, lax.all_gather(near_rows, "feat", axis=0, tiled=True))
    reduced = (grad_rows.astype(jnp.float32) - coupled).astype(jnp.bfloat16)
    piece = lax.all_gather(reduced, "feat", axis=0, tiled=True)
    whitened_acc = contract_rows(inverse_rows, piece)
    carried_acc = contract_rows(carry_rows, piece)
    whitened = whitened_acc.astype(jnp.bfloat16)
    carried = carried_acc.astype(jnp.bfloat16)
    local_term = block_apply(whitened, out_inv, False)
    middle = block_apply(carried, out_inv, False).astype(jnp.bfloat16)
    middle_from_below = from_behind(middle, "layer", 1)
    incoming = block_apply(middle_from_below, psi_from_below, False)
    return (local_term - incoming).astype(jnp.bfloat16)[None]


def solution(mesh):
    return jax.shard_map(
        local,
        mesh=mesh,
        in_specs=(
            P("layer", "feat", None),
            P("layer", "feat", None),
            P("layer", "feat", None),
            P("layer", "feat", None),
            P("layer", None, None, None),
            P("layer", None, None, None),
        ),
        out_specs=P("layer", "feat", None),
        check_vma=False,
    )
```

profile of v0, /device:TPU:1, one launch (start us, length us, event | category | flops | bytes accessed | tf_op | source)
XLA Modules:
  0.0 296.4 jit_solution(8207980276232798761)
XLA Ops:
  6.5 0.0 copy-start
  6.5 0.0 copy-start.4
  6.5 0.0 copy-start.2
  6.5 0.0 all-gather.3.cloned.1.call-start
  6.5 5.3 %collective-permute-start = (bf16[80,2560]{1,0:T(8,128)(2,1)}, bf16[80,2560]{1,0:T(8,128)(2,1)S(1)}, u32[]{:S(2)}, u32[]{:S(2)}) collective-permute-start(bf16[80,2560]{1,0:T(8,128)(2,1)} %bitcast.72), channel_id=1, source_target_pairs={{32,0},{64,32},{96,64},{128,96},{160,128},{192,160},{224,192},{33,... | collective-permute-start | bytes 1228808 | tf_op jit(solution)/shard_map/ppermute | solution.py:10
  11.8 5.2 %collective-permute-done = bf16[80,2560]{1,0:T(8,128)(2,1)S(1)} collective-permute-done((bf16[80,2560]{1,0:T(8,128)(2,1)}, bf16[80,2560]{1,0:T(8,128)(2,1)S(1)}, u32[]{:S(2)}, u32[]{:S(2)}) %collective-permute-start) | collective-permute-done | bytes 409632 | tf_op jit(solution)/shard_map/ppermute | solution.py:10
  17.0 1.7 fusion.6
  18.7 0.8 copy.41
  19.5 0.0 all-gather.3.cloned.1.call-update
  19.5 0.0 all-gather.5.cloned.1.call-start
  19.6 124.4 %all-gather.3.cloned.1.call-done = bf16[2560,2560]{1,0:T(8,128)(2,1)} async-done(((bf16[80,2560]{1,0:T(8,128)(2,1)}), bf16[2560,2560]{1,0:T(8,128)(2,1)}) %all-gather.3.cloned.1.call-update) | async-done | bytes 13107216 | tf_op jit(solution)/shard_map/all_gather | solution.py:37
  144.0 8.0 %fusion.1 = bf16[80,2560]{1,0:T(8,128)(2,1)} fusion(bf16[2560,2560]{1,0:T(8,128)(2,1)} %all-gather.3.cloned.1.call-done, bf16[1,80,2560]{2,1,0:T(8,128)(2,1)} %param.8, bf16[1,80,2560]{2,1,0:T(8,128)(2,1)} %param.6), kind=kOutput, calls=%fused_computation.2 | convolution fusion | flops 1049190400 | bytes 14336000 | tf_op jit(solution)/shard_map/dot_general | solution.py:24
  152.0 0.0 copy-start.3
  152.0 0.0 all-gather.5.cloned.1.call-update
  152.0 0.0 copy-done.4
  152.0 4.2 %collective-permute-start.2 = (bf16[20,128,128]{2,1,0:T(8,128)(2,1)S(1)}, bf16[20,128,128]{2,1,0:T(8,128)(2,1)S(1)}, u32[]{:S(2)}, u32[]{:S(2)}) collective-permute-start(bf16[20,128,128]{2,1,0:T(8,128)(2,1)S(1)} %bitcast.70), channel_id=1, source_target_pairs={{0,32},{32,64},{64,96},{96,128},{128,160},{160,192},{192,224},{1,3... | collective-permute-start | bytes 1966088 | tf_op jit(solution)/shard_map/ppermute | solution.py:10
  156.2 115.3 %all-gather.5.cloned.1.call-done = bf16[2560,2560]{1,0:T(8,128)(2,1)} async-done(((bf16[80,2560]{1,0:T(8,128)(2,1)}), bf16[2560,2560]{1,0:T(8,128)(2,1)}) %all-gather.5.cloned.1.call-update) | async-done | bytes 13107216 | tf_op jit(solution)/shard_map/all_gather | solution.py:39
  271.5 0.0 copy-done.2
  271.5 7.3 %fusion.4 = bf16[10,20,8,128]{3,2,1,0:T(8,128)(2,1)S(1)} fusion(bf16[2560,2560]{1,0:T(8,128)(2,1)} %all-gather.5.cloned.1.call-done, bf16[1,80,2560]{2,1,0:T(8,128)(2,1)S(1)} %copy-done.2), kind=kOutput, calls=%fused_computation.10 | convolution fusion | flops 1048780800 | bytes 13926400 | tf_op jit(solution)/shard_map/dot_general | solution.py:24
  278.7 0.0 copy-done
  278.7 0.4 fusion.7
  279.1 0.1 copy.40
  279.2 4.0 %collective-permute-start.1 = (bf16[80,2560]{1,0:T(8,128)(2,1)S(1)}, bf16[80,2560]{1,0:T(8,128)(2,1)S(1)}, u32[]{:S(2)}, u32[]{:S(2)}) collective-permute-start(bf16[80,2560]{1,0:T(8,128)(2,1)S(1)} %bitcast.71), channel_id=1, source_target_pairs={{0,32},{32,64},{64,96},{96,128},{128,160},{160,192},{192,224},{1,3... | collective-permute-start | bytes 1228808 | tf_op jit(solution)/shard_map/ppermute | solution.py:10
  283.2 0.0 copy-done.3
  283.2 0.0 copy-done.1
  283.2 2.4 fusion.3
  285.6 0.4 fusion.9
  286.0 0.0 collective-permute-done.2
  286.0 2.1 collective-permute-done.1
  288.1 0.4 fusion.5
  288.5 0.1 copy.15
  288.6 1.0 convert_element_type.66
  (1 shorter events, 0.0 us)
Async XLA Ops:
  6.5 272.2 %copy-start = (bf16[1,20,128,128]{3,2,1,0:T(8,128)(2,1)S(1)}, bf16[1,20,128,128]{3,2,1,0:T(8,128)(2,1)}, u32[]{:S(2)}) copy-start(bf16[1,20,128,128]{3,2,1,0:T(8,128)(2,1)} %param.10) | copy-start | bytes 1966084
  6.5 145.5 %copy-start.4 = (bf16[1,20,128,128]{3,2,1,0:T(8,128)(2,1)S(1)}, bf16[1,20,128,128]{3,2,1,0:T(8,128)(2,1)}, u32[]{:S(2)}) copy-start(bf16[1,20,128,128]{3,2,1,0:T(8,128)(2,1)} %param.11) | copy-start | bytes 1966084
  6.5 264.9 %copy-start.2 = (bf16[1,80,2560]{2,1,0:T(8,128)(2,1)S(1)}, bf16[1,80,2560]{2,1,0:T(8,128)(2,1)}, u32[]{:S(2)}) copy-start(bf16[1,80,2560]{2,1,0:T(8,128)(2,1)} %param.9) | copy-start | bytes 1228804
  6.5 137.4 %all-gather.3.cloned.1.call-start = ((), (), s32[]{:S(2)}) async-start(), calls=%async_computation | async-start | bytes 13516800 | tf_op jit(solution)/shard_map/all_gather | solution.py:37
  6.5 10.5 %collective-permute-start = (bf16[80,2560]{1,0:T(8,128)(2,1)}, bf16[80,2560]{1,0:T(8,128)(2,1)S(1)}, u32[]{:S(2)}, u32[]{:S(2)}) collective-permute-start(bf16[80,2560]{1,0:T(8,128)(2,1)} %bitcast.72), channel_id=1, source_target_pairs={{32,0},{64,32},{96,64},{128,96},{160,128},{192,160},{224,192},{33,... | collective-permute-start | bytes 1228808 | tf_op jit(solution)/shard_map/ppermute | solution.py:10
  19.5 251.9 %all-gather.5.cloned.1.call-start = ((), (), s32[]{:S(2)}) async-start(), calls=%async_computation.1 | async-start | bytes 13516800 | tf_op jit(solution)/shard_map/all_gather | solution.py:39
  152.0 131.2 %copy-start.3 = (bf16[1,80,2560]{2,1,0:T(8,128)(2,1)S(1)}, bf16[1,80,2560]{2,1,0:T(8,128)(2,1)}, u32[]{:S(2)}) copy-start(bf16[1,80,2560]{2,1,0:T(8,128)(2,1)} %param.7) | copy-start | bytes 1228804
  152.0 134.0 %collective-permute-start.2 = (bf16[20,128,128]{2,1,0:T(8,128)(2,1)S(1)}, bf16[20,128,128]{2,1,0:T(8,128)(2,1)S(1)}, u32[]{:S(2)}, u32[]{:S(2)}) collective-permute-start(bf16[20,128,128]{2,1,0:T(8,128)(2,1)S(1)} %bitcast.70), channel_id=1, source_target_pairs={{0,32},{32,64},{64,96},{96,128},{128,160},{160,192},{192,224},{1,3... | collective-permute-start | bytes 1966088 | tf_op jit(solution)/shard_map/ppermute | solution.py:10
  271.5 11.8 %copy-start.1 = (bf16[2560,2560]{1,0:T(8,128)(2,1)S(1)}, bf16[2560,2560]{1,0:T(8,128)(2,1)}, u32[]{:S(2)}) copy-start(bf16[2560,2560]{1,0:T(8,128)(2,1)} %all-gather.5.cloned.1.call-done) | copy-start | bytes 39321604
  279.2 8.9 %collective-permute-start.1 = (bf16[80,2560]{1,0:T(8,128)(2,1)S(1)}, bf16[80,2560]{1,0:T(8,128)(2,1)S(1)}, u32[]{:S(2)}, u32[]{:S(2)}) collective-permute-start(bf16[80,2560]{1,0:T(8,128)(2,1)S(1)} %bitcast.71), channel_id=1, source_target_pairs={{0,32},{32,64},{64,96},{96,128},{128,160},{160,192},{192,224},{1,3... | collective-permute-start | bytes 1228808 | tf_op jit(solution)/shard_map/ppermute | solution.py:10
Sparse Core Ops, SparseCore 0:
  19.7 124.2 all-gather.2
  152.1 119.3 all-gather.4
where the time goes:
time: 297 us; the launch traced here: 296 us
  waiting for transfers between devices  247 us (83%)
  matrix products  20.4 us (7%)
  starting transfers between devices  13.5 us (5%)
  between operations  13.5 us (5%)
    all_gather x1, waiting for transfers between devices, local(): lax.all_gather(near_rows, 'feat', axis=0, tiled=True)  124 us
    all_gather x1, waiting for transfers between devices, local(): piece = lax.all_gather(reduced, 'feat', axis=0, tiled=True)  115 us
    dot_general x3, matrix products, contract_rows(): return jnp.dot(factor, piece, preferred_element_type=jnp.float32)  17.6 us
    ppermute x3, starting transfers between devices, from_behind(): return lax.ppermute(x, axis, pairs)  13.5 us
    ppermute x3, waiting for transfers between devices, from_behind(): return lax.ppermute(x, axis, pairs)  7.29 us
  transfers between devices with their start and end apart: 5, of which 4 were waited for; matrix products, arithmetic and copies ran while one was open for 4% of the time, Pallas kernels for 0%

commit v1 on v0

--- a/solution.py
+++ b/solution.py
@@ -2,6 +2,14 @@
 import jax.numpy as jnp
 from jax import lax
 from jax.sharding import PartitionSpec as P
+
+
+def settle_domain_now(panel, row_dim):
+    val = jnp.concatenate(
+        lax.all_to_all(jnp.stack([panel for _ in range(lax.axis_size("feat"))], 0), "feat", 0, 0),
+        row_dim,
+    )
+    return val
 
 
 def from_behind(x, axis, by):
@@ -34,7 +42,7 @@
     psi_from_below = from_behind(out_psi, "layer", 1)
     from_above = from_behind(grad_rows, "layer", -1)
     near_rows = block_apply(from_above, out_psi, True).astype(jnp.bfloat16)
-    coupled = contract_rows(coupling_rows, lax.all_gather(near_rows, "feat", axis=0, tiled=True))
+    coupled = contract_rows(coupling_rows, settle_domain_now(near_rows, 0))
     reduced = (grad_rows.astype(jnp.float32) - coupled).astype(jnp.bfloat16)
     piece = lax.all_gather(reduced, "feat", axis=0, tiled=True)
     whitened_acc = contract_rows(inverse_rows, piece)

time: 297 us -> 470 us (1.58)
  blocking collectives: 0 us -> 294 us
  waiting for transfers between devices: 247 us -> 123 us
  local copies, waits for them, and re-layouts: 2.04 us -> 7.45 us
  matrix products: 20.4 us -> 15.5 us
    all_to_all x0 -> x1, blocking collectives: none -> 294 us  [settle_domain_now(): lax.all_to_all(jnp.stack([panel for _ in range(lax.axis_size('feat'))], 0...]
    all_gather x1 -> x0, waiting for transfers between devices: 124 us -> none  [local(): lax.all_gather(near_rows, 'feat', axis=0, tiled=True)]
    another operation x0 -> x1, local copies, waits for them, and re-layouts: none -> 6.16 us  [settle_domain_now(): jnp.stack([panel for _ in range(lax.axis_size('feat'))], 0)]
    dot_general x3, matrix products: 17.6 us -> 12.8 us  [contract_rows(): return jnp.dot(factor, piece, preferred_element_type=jnp.float32)]
  transfers between devices with their start and end apart: 5 -> 4, of which waited for: 4 -> 3; matrix products, arithmetic and copies ran while one was open for 4% -> 2% of each run, Pallas kernels for 0% -> 0%
where the time goes in v1:
time: 470 us
  blocking collectives  294 us (63%)
  waiting for transfers between devices  123 us (26%)
  starting transfers between devices  16.2 us (3%)
  matrix products  15.5 us (3%)
  between operations  13.5 us (3%)
  local copies, waits for them, and re-layouts  7.45 us (2%)
    all_to_all x1, blocking collectives, settle_domain_now(): lax.all_to_all(jnp.stack([panel for _ in range(lax.axis_size('feat'))], 0...  294 us
    all_gather x1, waiting for transfers between devices, local(): piece = lax.all_gather(reduced, 'feat', axis=0, tiled=True)  116 us
    ppermute x3, starting transfers between devices, from_behind(): return lax.ppermute(x, axis, pairs)  16.2 us
    dot_general x3, matrix products, contract_rows(): return jnp.dot(factor, piece, preferred_element_type=jnp.float32)  12.8 us
  transfers between devices with their start and end apart: 4, of which 3 were waited for; matrix products, arithmetic and copies ran while one was open for 2% of the time, Pallas kernels for 0%

profile of v1, /device:TPU:1, one launch (start us, length us, event | category | flops | bytes accessed | tf_op | source)
XLA Modules:
  0.0 469.9 jit_solution(1412267083530222147)
XLA Ops:
  6.5 0.0 copy-start
  6.5 0.0 all-gather.2.cloned.1.call-start
  6.5 5.3 %collective-permute-start = (bf16[80,2560]{1,0:T(8,128)(2,1)}, bf16[80,2560]{1,0:T(8,128)(2,1)S(1)}, u32[]{:S(2)}, u32[]{:S(2)}) collective-permute-start(bf16[80,2560]{1,0:T(8,128)(2,1)} %bitcast.74), channel_id=1, source_target_pairs={{32,0},{64,32},{96,64},{128,96},{160,128},{192,160},{224,192},{33,... | collective-permute-start | bytes 1228808 | tf_op jit(solution)/shard_map/ppermute | solution.py:18
  11.8 5.2 %collective-permute-done = bf16[80,2560]{1,0:T(8,128)(2,1)S(1)} collective-permute-done((bf16[80,2560]{1,0:T(8,128)(2,1)}, bf16[80,2560]{1,0:T(8,128)(2,1)S(1)}, u32[]{:S(2)}, u32[]{:S(2)}) %collective-permute-start) | collective-permute-done | bytes 409632 | tf_op jit(solution)/shard_map/ppermute | solution.py:18
  17.0 1.7 fusion.6
  18.7 0.1 copy.41
  18.8 6.2 %stack.2 = bf16[32,80,2560]{2,1,0:T(8,128)(2,1)} broadcast(bf16[80,2560]{1,0:T(8,128)(2,1)S(1)} %bitcast.71), dimensions={1,2} | broadcast | bytes 13516800 | tf_op jit(solution)/shard_map/stack | solution.py:9
  24.9 0.0 copy-start.4
  24.9 293.7 %all_to_all.5 = bf16[32,80,2560]{2,1,0:T(8,128)(2,1)S(1)} all-to-all(bf16[32,80,2560]{2,1,0:T(8,128)(2,1)} %stack.2), channel_id=1, replica_groups=mesh['layer'=8,'feat'=32] {'feat'}, dimensions={0} | all-to-all | bytes 26214400 | tf_op jit(solution)/shard_map/all_to_all | solution.py:9
  318.6 0.0 copy-start.5
  318.6 0.0 copy-done.4
  318.6 0.0 copy-done.6
  318.6 3.1 fusion.1
  321.8 0.0 all-gather.2.cloned.1.call-update
  321.8 0.0 copy-done.5
  321.8 6.9 %collective-permute-start.2 = (bf16[20,128,128]{2,1,0:T(8,128)(2,1)S(1)}, bf16[20,128,128]{2,1,0:T(8,128)(2,1)S(1)}, u32[]{:S(2)}, u32[]{:S(2)}) collective-permute-start(bf16[20,128,128]{2,1,0:T(8,128)(2,1)S(1)} %bitcast.72), channel_id=1, source_target_pairs={{0,32},{32,64},{64,96},{96,128},{128,160},{160,192},{192,224},{1,3... | collective-permute-start | bytes 1966088 | tf_op jit(solution)/shard_map/ppermute | solution.py:18
  328.7 116.2 %all-gather.2.cloned.1.call-done = bf16[2560,2560]{1,0:T(8,128)(2,1)} async-done(((bf16[80,2560]{1,0:T(8,128)(2,1)}), bf16[2560,2560]{1,0:T(8,128)(2,1)}) %all-gather.2.cloned.1.call-update) | async-done | bytes 13107216 | tf_op jit(solution)/shard_map/all_gather | solution.py:47
  444.9 0.0 copy-done.2
  444.9 7.3 %fusion.4 = bf16[10,20,8,128]{3,2,1,0:T(8,128)(2,1)S(1)} fusion(bf16[2560,2560]{1,0:T(8,128)(2,1)} %all-gather.2.cloned.1.call-done, bf16[1,80,2560]{2,1,0:T(8,128)(2,1)S(1)} %copy-done.2), kind=kOutput, calls=%fused_computation.10 | convolution fusion | flops 1048780800 | bytes 13926400 | tf_op jit(solution)/shard_map/dot_general | solution.py:32
  452.2 0.0 copy-done
  452.2 0.4 fusion.7
  452.5 0.1 copy.40
  452.6 4.0 collective-permute-start.1
  456.6 0.0 copy-done.3
  456.7 0.0 copy-done.1
  456.7 2.4 fusion.3
  459.0 0.4 fusion.9
  459.4 0.0 collective-permute-done.2
  459.4 2.1 collective-permute-done.1
  461.5 0.4 fusion.5
  461.9 0.1 copy.15
  462.0 1.0 convert_element_type.68
  (4 shorter events, 0.0 us)
Async XLA Ops:
  6.5 445.6 %copy-start = (bf16[1,20,128,128]{3,2,1,0:T(8,128)(2,1)S(1)}, bf16[1,20,128,128]{3,2,1,0:T(8,128)(2,1)}, u32[]{:S(2)}) copy-start(bf16[1,20,128,128]{3,2,1,0:T(8,128)(2,1)} %param.10) | copy-start | bytes 1966084
  6.5 438.4 %all-gather.2.cloned.1.call-start = ((), (), s32[]{:S(2)}) async-start(), calls=%async_computation.1 | async-start | bytes 13516800 | tf_op jit(solution)/shard_map/all_gather | solution.py:47
  6.5 10.5 %collective-permute-start = (bf16[80,2560]{1,0:T(8,128)(2,1)}, bf16[80,2560]{1,0:T(8,128)(2,1)S(1)}, u32[]{:S(2)}, u32[]{:S(2)}) collective-permute-start(bf16[80,2560]{1,0:T(8,128)(2,1)} %bitcast.74), channel_id=1, source_target_pairs={{32,0},{64,32},{96,64},{128,96},{160,128},{192,160},{224,192},{33,... | collective-permute-start | bytes 1228808 | tf_op jit(solution)/shard_map/ppermute | solution.py:18
  24.9 293.7 %copy-start.4 = (bf16[1,80,2560]{2,1,0:T(8,128)(2,1)S(1)}, bf16[1,80,2560]{2,1,0:T(8,128)(2,1)}, u32[]{:S(2)}) copy-start(bf16[1,80,2560]{2,1,0:T(8,128)(2,1)} %param.8) | copy-start | bytes 1228804
  24.9 293.7 %copy-start.6 = (bf16[1,80,2560]{2,1,0:T(8,128)(2,1)S(1)}, bf16[1,80,2560]{2,1,0:T(8,128)(2,1)}, u32[]{:S(2)}) copy-start(bf16[1,80,2560]{2,1,0:T(8,128)(2,1)} %param.6) | copy-start | bytes 1228804
  318.6 3.2 copy-start.5
  318.6 126.3 %copy-start.2 = (bf16[1,80,2560]{2,1,0:T(8,128)(2,1)S(1)}, bf16[1,80,2560]{2,1,0:T(8,128)(2,1)}, u32[]{:S(2)}) copy-start(bf16[1,80,2560]{2,1,0:T(8,128)(2,1)} %param.9) | copy-start | bytes 1228804
  321.8 134.9 %copy-start.3 = (bf16[1,80,2560]{2,1,0:T(8,128)(2,1)S(1)}, bf16[1,80,2560]{2,1,0:T(8,128)(2,1)}, u32[]{:S(2)}) copy-start(bf16[1,80,2560]{2,1,0:T(8,128)(2,1)} %param.7) | copy-start | bytes 1228804
  321.8 137.6 %collective-permute-start.2 = (bf16[20,128,128]{2,1,0:T(8,128)(2,1)S(1)}, bf16[20,128,128]{2,1,0:T(8,128)(2,1)S(1)}, u32[]{:S(2)}, u32[]{:S(2)}) collective-permute-start(bf16[20,128,128]{2,1,0:T(8,128)(2,1)S(1)} %bitcast.72), channel_id=1, source_target_pairs={{0,32},{32,64},{64,96},{96,128},{128,160},{160,192},{192,224},{1,3... | collective-permute-start | bytes 1966088 | tf_op jit(solution)/shard_map/ppermute | solution.py:18
  444.9 11.8 %copy-start.1 = (bf16[2560,2560]{1,0:T(8,128)(2,1)S(1)}, bf16[2560,2560]{1,0:T(8,128)(2,1)}, u32[]{:S(2)}) copy-start(bf16[2560,2560]{1,0:T(8,128)(2,1)} %all-gather.2.cloned.1.call-done) | copy-start | bytes 39321604
  452.6 8.9 %collective-permute-start.1 = (bf16[80,2560]{1,0:T(8,128)(2,1)S(1)}, bf16[80,2560]{1,0:T(8,128)(2,1)S(1)}, u32[]{:S(2)}, u32[]{:S(2)}) collective-permute-start(bf16[80,2560]{1,0:T(8,128)(2,1)S(1)} %bitcast.73), channel_id=1, source_target_pairs={{0,32},{32,64},{64,96},{96,128},{128,160},{160,192},{192,224},{1,3... | collective-permute-start | bytes 1228808 | tf_op jit(solution)/shard_map/ppermute | solution.py:18
Sparse Core Ops, SparseCore 0:
  321.9 122.9 all-gather.1
